TPU v7x, 32 devices: a whole 2x2x4 slice. The times are simulated.
32 devices in a mesh: amp: 4 (over y, core), own: 8 (over z, x).
Axes of the slice: x: 2, y: 2, z: 4, core: 2. Of those that a mesh axis runs over, the one named last changes fastest.
Arguments:
- amplitudes: bfloat16 [32, 2304, 192], P('own', None, 'amp'), may hold values from -6 to 6
- integrals: bfloat16 [32, 1152, 2304], P('own'), as said below
- occ_irrep: int32 [34], replicated, may hold values from 0 to 7, as said below
- tile_irrep: int32 [18], replicated, may hold values from 0 to 7, as said below
Outputs:
- cycle_term: bfloat16 [2304, 2304], P(('amp', 'own'))
Inputs may be any that keep to these rules, and one draw needn't show every extreme that they name: `occ_irrep`: labels of the D2h group, combined by XOR; every label occurs, and all labels occur equally often up to one. `tile_irrep`: labels of the D2h group, combined by XOR; every label occurs, and all labels occur equally often up to one, so some label has exactly 3 tiles. integrals[k, c, (j, b)] is zero unless the labels of k, c, j and b combine by XOR to 0.
All inputs are finite; a program needn't handle non-finite values.
Results may differ from a plain program's by a relative error of at most 0.001.
Values may be sent and summed in bfloat16 or wider, within the bound.
A program may use at most 128 MiB of HBM per device.

v0:
```python
import jax
import jax.numpy as jnp
from jax import lax
from jax.sharding import PartitionSpec as P

V = 1152
TILE = 64
NI = 2


def tile_ranks(tile_irrep):
    count = tile_irrep.shape[0]
    index = jnp.arange(count, dtype=jnp.int32)
    same = (tile_irrep[:, None] == tile_irrep[None, :]) & (index[None, :] < index[:, None])
    return jnp.sum(same.astype(jnp.int32), axis=1)


def shards(amplitudes, integrals, occ_irrep, tile_irrep):
    amp_index = lax.axis_index("amp")
    own_index = lax.axis_index("own")
    n_amp = lax.axis_size("amp")
    n_own = lax.axis_size("own")
    regrouped = lax.all_to_all(amplitudes, "amp", split_axis=1, concat_axis=2, tiled=True)
    k_local, rows, packed_width = regrouped.shape
    slot_count = packed_width // TILE
    virt_lab = jnp.repeat(tile_irrep, TILE)
    row_all = jnp.bitwise_xor(jnp.repeat(occ_irrep[:NI], V), jnp.tile(virt_lab, NI))
    row_lab = lax.dynamic_slice_in_dim(row_all, amp_index * rows, rows)
    k_lab = lax.dynamic_slice_in_dim(occ_irrep, NI + own_index * k_local, k_local)
    wanted = jnp.bitwise_xor(k_lab[:, None], row_lab[None, :])
    ranks = tile_ranks(tile_irrep)
    slot_ids = jnp.arange(slot_count, dtype=jnp.int32)
    select = (tile_irrep[None, None, None, :] == wanted[:, :, None, None]) & (
        ranks[None, None, None, :] == slot_ids[None, None, :, None]
    )
    pieces = regrouped.reshape(k_local, rows, slot_count, TILE)
    dense = jnp.einsum(
        "krjt,krje->krte", select.astype(jnp.bfloat16), pieces, preferred_element_type=jnp.float32
    )
    masked = dense.reshape(k_local, rows, V).astype(jnp.bfloat16)
    summed = lax.psum_scatter(
        jnp.einsum("kmc,kcn->mn", masked, integrals, preferred_element_type=jnp.float32),
        "own",
        scatter_dimension=0,
        tiled=True,
    )
    share = summed.shape[0]
    blocks = summed.reshape(share, n_amp, n_own, share)
    moved = lax.all_to_all(
        lax.all_to_all(blocks, "amp", split_axis=1, concat_axis=1, tiled=True),
        "own",
        split_axis=2,
        concat_axis=2,
        tiled=True,
    )
    mirrored = jnp.transpose(moved, (3, 1, 2, 0)).reshape(share, NI * V)
    return (summed + mirrored).astype(jnp.bfloat16)


def solution(mesh):
    return jax.shard_map(
        shards,
        mesh=mesh,
        in_specs=(P("own", None, "amp"), P("own", None, None), P(), P()),
        out_specs=P(("amp", "own"), None),
        check_vma=False,
    )
```

profile of v0, /device:TPU:0, one launch (start us, length us, event | category | flops | bytes accessed | tf_op | source)
XLA Modules:
  0.0 252.3 jit_solution(9332235532349839505)
XLA Ops:
  6.5 3.6 %copy.25 = bf16[4,2304,48]{2,0,1:T(4,128)(2,1)S(1)} copy(bf16[4,2304,48]{1,2,0:T(8,128)(2,1)} %param.4) | data formatting | bytes 1769472 | tf_op args[0]
  10.1 4.6 %reshape.80 = bf16[4,2,55296]{2,1,0:T(2,128)(2,1)} reshape(bf16[2304,4,48]{2,1,0:T(4,128)(2,1)S(1)} %bitcast.18) | data formatting | bytes 1769472
  14.8 4.2 %all-to-all-start = ((bf16[4,2,55296]{2,1,0:T(2,128)(2,1)}), bf16[4,2,55296]{2,1,0:T(2,128)(2,1)S(1)}, u32[]{:S(2)}, u32[]{:S(2)}) async-start(bf16[4,2,55296]{2,1,0:T(2,128)(2,1)} %reshape.80), calls=%async_computation | async-start | bytes 1769472 | tf_op jit(solution)/shard_map/all_to_all | solution.py:23
  19.0 0.2 convert_reduce_fusion
  19.3 0.1 tile.8
  19.3 0.1 dynamic_slice.6
  19.5 0.1 dynamic_slice.7
  19.7 1.1 broadcast_compare_fusion
  20.8 10.9 %all-to-all-done = bf16[4,2,55296]{2,1,0:T(2,128)(2,1)S(1)} async-done(((bf16[4,2,55296]{2,1,0:T(2,128)(2,1)}), bf16[4,2,55296]{2,1,0:T(2,128)(2,1)S(1)}, u32[]{:S(2)}, u32[]{:S(2)}) %all-to-all-start) | async-done | bytes 884768 | tf_op jit(solution)/shard_map/all_to_all | solution.py:23
  31.7 2.4 reshape.81
  34.1 1.5 copy.27
  35.6 1.5 copy.28
  37.1 11.1 %convolution_convert_fusion = bf16[4,576,18,64]{3,2,1,0:T(8,128)(2,1)} fusion(bf16[4,576,3,64]{3,2,1,0:T(4,128)(2,1)S(1)} %copy.28, pred[3,18]{1,0:T(4,128)(4,1)S(1)} %iota_compare_fusion.1, pred[4,576,18]{2,1,0:T(8,128)(4,1)} %broadcast_compare_fusion), kind=kOutput, calls=%fused_computation | convolution fusion | flops 18703872 | bytes 6234678 | tf_op jit(solution)/shard_map/krjt,krje->krte/dot_general | solution.py:37
  48.2 15.5 %copy.29 = bf16[4,576,18,64]{1,3,2,0:T(8,128)(2,1)} copy(bf16[4,576,18,64]{3,2,1,0:T(8,128)(2,1)} %convolution_convert_fusion) | data formatting | bytes 10616832 | tf_op jit(solution)/shard_map/convert_element_type | solution.py:40
  63.7 19.2 %convolution_bitcast_fusion = f32[576,2304]{1,0:T(8,128)} fusion(bf16[4,576,1152]{1,2,0:T(8,128)(2,1)} %bitcast.19, bf16[4,1152,2304]{2,1,0:T(8,128)(2,1)} %param.5), kind=kOutput, calls=%fused_computation.1 | convolution fusion | flops 12230590464 | bytes 31850496 | tf_op jit(solution)/shard_map/kmc,kcn->mn/dot_general | solution.py:42
  82.9 105.3 %reduce-scatter.2.cloned.1.call-done = f32[72,2304]{1,0:T(8,128)} async-done(((f32[576,2304]{1,0:T(8,128)}), f32[72,2304]{1,0:T(8,128)}) %reduce-scatter.2.cloned.1.call-update) | async-done | bytes 663568 | tf_op jit(solution)/shard_map/reduce_scatter | solution.py:41
  188.2 2.3 reshape.77
  190.5 0.9 copy.31
  191.4 18.4 %all_to_all.25 = f32[72,4,8,72]{0,2,3,1:T(8,128)S(1)} all-to-all(f32[72,4,8,72]{0,2,3,1:T(8,128)S(1)} %copy.31), channel_id=1, replica_groups=mesh['amp'=4,'own'=8] {'amp'}, dimensions={1} | all-to-all | bytes 1327104 | tf_op jit(solution)/shard_map/all_to_all | solution.py:50
  209.8 0.8 copy.32
  210.6 32.7 %all_to_all.26 = f32[72,4,8,72]{0,1,3,2:T(4,128)S(1)} all-to-all(f32[72,4,8,72]{0,1,3,2:T(4,128)S(1)} %copy.32), channel_id=1, replica_groups=mesh['amp'=4,'own'=8] {'own'}, dimensions={2} | all-to-all | bytes 1327104 | tf_op jit(solution)/shard_map/all_to_all | solution.py:49
  243.3 0.7 copy.33
  244.0 0.6 reshape.78
  244.7 0.8 add_convert_fusion
  (13 shorter events, 0.3 us)
Async XLA Ops:
  10.1 8.9 %copy-start.1 = (s32[18]{0:T(128)S(1)}, s32[18]{0:T(128)}, u32[]{:S(2)}) copy-start(s32[18]{0:T(128)} %param.7) | copy-start | bytes 220
  10.1 9.2 %copy-start.2 = (s32[34]{0:T(128)S(1)}, s32[34]{0:T(128)}, u32[]{:S(2)}) copy-start(s32[34]{0:T(128)} %param.6) | copy-start | bytes 412
  14.8 16.9 %all-to-all-start = ((bf16[4,2,55296]{2,1,0:T(2,128)(2,1)}), bf16[4,2,55296]{2,1,0:T(2,128)(2,1)S(1)}, u32[]{:S(2)}, u32[]{:S(2)}) async-start(bf16[4,2,55296]{2,1,0:T(2,128)(2,1)} %reshape.80), calls=%async_computation | async-start | bytes 1769472 | tf_op jit(solution)/shard_map/all_to_all | solution.py:23
  19.0 169.2 %reduce-scatter.2.cloned.1.call-start = ((), (), s32[]{:S(2)}) async-start(), calls=%async_computation.4 | async-start | bytes 5971968 | tf_op jit(solution)/shard_map/reduce_scatter | solution.py:41
  243.3 1.3 copy-start
Sparse Core Ops, SparseCore 0:
  83.0 105.1 reduce-scatter.1
where the time goes:
time: 253 us; the launch traced here: 252 us
  waiting for transfers between devices  116 us (46%)
  blocking collectives  51.1 us (20%)
  local copies, waits for them, and re-layouts  34.7 us (14%)
  matrix products  30.3 us (12%)
  between operations  13.5 us (5%)
  starting transfers between devices  4.24 us (2%)
    reduce_scatter x1, waiting for transfers between devices, shards(): lax.psum_scatter(jnp.einsum('kmc,kcn->mn', masked, integrals, preferred_e...  105 us
    all_to_all x1, blocking collectives, shards(): lax.all_to_all(lax.all_to_all(blocks, 'amp', split_axis=1, concat_axis=1,...  32.7 us
    dot_general x1, matrix products, shards(): jnp.einsum('kmc,kcn->mn', masked, integrals, preferred_element_type=jnp.f...  19.2 us
    all_to_all x1, blocking collectives, shards(): lax.all_to_all(blocks, 'amp', split_axis=1, concat_axis=1, tiled=True)  18.4 us
    convert_element_type x1, local copies, waits for them, and re-layouts, shards(): masked = dense.reshape(k_local, rows, V).astype(jnp.bfloat16)  15.5 us
    dot_general x1, matrix products, shards(): jnp.einsum('krjt,krje->krte', select.astype(jnp.bfloat16), pieces, prefer...  11.1 us
    all_to_all x1, waiting for transfers between devices, shards(): lax.all_to_all(amplitudes, 'amp', split_axis=1, concat_axis=2, tiled=True)  10.9 us
    unnamed x9, local copies, waits for them, and re-layouts  10.6 us
  transfers between devices with their start and end apart: 2, of which 2 were waited for; matrix products, arithmetic and copies ran while one was open for 1% of the time, Pallas kernels for 0%

commit v1 on v0

--- a/solution.py
+++ b/solution.py
@@ -20,7 +20,10 @@
     own_index = lax.axis_index("own")
     n_amp = lax.axis_size("amp")
     n_own = lax.axis_size("own")
-    regrouped = lax.all_to_all(amplitudes, "amp", split_axis=1, concat_axis=2, tiled=True)
+    regrouped = jnp.concatenate(
+        lax.all_to_all(jnp.stack(jnp.split(amplitudes, lax.axis_size("amp"), axis=1)), "amp", 0, 0),
+        axis=2,
+    )
     k_local, rows, packed_width = regrouped.shape
     slot_count = packed_width // TILE
     virt_lab = jnp.repeat(tile_irrep, TILE)

time: 253 us -> 245 us (0.968)
  local copies, waits for them, and re-layouts: 34.7 us -> 24.1 us
    unnamed x9 -> x6, local copies, waits for them, and re-layouts: 10.6 us -> 0.02 us
    another operation x0 -> x2, local copies, waits for them, and re-layouts: none -> 2.96 us  [the longest x1 1.52 us: shards(): pieces = regrouped.reshape(k_local, rows, slot_count, TILE)]
where the time goes in v1:
time: 245 us; the launch traced here: 244 us
  waiting for transfers between devices  117 us (48%)
  blocking collectives  51.1 us (21%)
  matrix products  30.3 us (12%)
  local copies, waits for them, and re-layouts  24.1 us (10%)
  between operations  13.5 us (6%)
  starting transfers between devices  4.24 us (2%)
  other arithmetic  3.42 us (1%)
    reduce_scatter x1, waiting for transfers between devices, shards(): lax.psum_scatter(jnp.einsum('kmc,kcn->mn', masked, integrals, preferred_e...  105 us
    all_to_all x1, blocking collectives, shards(): lax.all_to_all(lax.all_to_all(blocks, 'amp', split_axis=1, concat_axis=1,...  32.7 us
    dot_general x1, matrix products, shards(): jnp.einsum('kmc,kcn->mn', masked, integrals, preferred_element_type=jnp.f...  19.2 us
    all_to_all x1, blocking collectives, shards(): lax.all_to_all(blocks, 'amp', split_axis=1, concat_axis=1, tiled=True)  18.4 us
    convert_element_type x1, local copies, waits for them, and re-layouts, shards(): masked = dense.reshape(k_local, rows, V).astype(jnp.bfloat16)  15.4 us
    all_to_all x1, waiting for transfers between devices, shards(): lax.all_to_all(jnp.stack(jnp.split(amplitudes, lax.axis_size('amp'), axis...  12 us
    dot_general x1, matrix products, shards(): jnp.einsum('krjt,krje->krte', select.astype(jnp.bfloat16), pieces, prefer...  11.1 us
  transfers between devices with their start and end apart: 2, of which 2 were waited for; matrix products, arithmetic and copies ran while one was open for 1% of the time, Pallas kernels for 0%

profile of v1, /device:TPU:0, one launch (start us, length us, event | category | flops | bytes accessed | tf_op | source)
XLA Modules:
  0.0 244.0 jit_solution(822453945313573416)
XLA Ops:
  6.5 1.4 slice_bitcast_fusion.3
  8.0 1.2 pad_maximum_fusion
  9.2 4.2 %all-to-all-start = ((bf16[4,4,576,48]{2,3,1,0:T(8,128)(2,1)}), bf16[4,4,576,48]{2,3,1,0:T(8,128)(2,1)S(1)}, u32[]{:S(2)}, u32[]{:S(2)}) async-start(bf16[4,4,576,48]{2,3,1,0:T(8,128)(2,1)} %pad_maximum_fusion), calls=%async_computation | async-start | bytes 1966080 | tf_op jit(solution)/shard_map/all_to_all | solution.py:24
  13.4 0.2 convert_reduce_fusion
  13.7 0.1 tile.8
  13.7 0.1 dynamic_slice.6
  13.8 0.1 broadcast_xor_fusion.1
  13.9 0.1 dynamic_slice.7
  14.1 1.1 broadcast_compare_fusion
  15.2 12.0 %all-to-all-done = bf16[4,4,576,48]{2,3,1,0:T(8,128)(2,1)S(1)} async-done(((bf16[4,4,576,48]{2,3,1,0:T(8,128)(2,1)}), bf16[4,4,576,48]{2,3,1,0:T(8,128)(2,1)S(1)}, u32[]{:S(2)}, u32[]{:S(2)}) %all-to-all-start) | async-done | bytes 884768 | tf_op jit(solution)/shard_map/all_to_all | solution.py:24
  27.2 0.1 copy.18
  27.3 1.5 copy.19
  28.8 11.1 %convolution_convert_fusion = bf16[4,576,18,64]{3,2,1,0:T(8,128)(2,1)} fusion(bf16[4,576,3,64]{3,2,1,0:T(4,128)(2,1)S(1)} %copy.19, pred[3,18]{1,0:T(4,128)(4,1)S(1)} %iota_compare_fusion.1, pred[4,576,18]{2,1,0:T(8,128)(4,1)} %broadcast_compare_fusion), kind=kOutput, calls=%fused_computation | convolution fusion | flops 18703872 | bytes 6234678 | tf_op jit(solution)/shard_map/krjt,krje->krte/dot_general | solution.py:40
  39.9 15.4 %copy.20 = bf16[4,576,18,64]{1,3,2,0:T(8,128)(2,1)} copy(bf16[4,576,18,64]{3,2,1,0:T(8,128)(2,1)} %convolution_convert_fusion) | data formatting | bytes 10616832 | tf_op jit(solution)/shard_map/convert_element_type | solution.py:43
  55.3 19.2 %convolution_bitcast_fusion = f32[576,2304]{1,0:T(8,128)} fusion(bf16[4,576,1152]{1,2,0:T(8,128)(2,1)} %bitcast.21, bf16[4,1152,2304]{2,1,0:T(8,128)(2,1)} %param.5), kind=kOutput, calls=%fused_computation.1 | convolution fusion | flops 12230590464 | bytes 31850496 | tf_op jit(solution)/shard_map/kmc,kcn->mn/dot_general | solution.py:45
  74.5 105.4 %reduce-scatter.2.cloned.1.call-done = f32[72,2304]{1,0:T(8,128)} async-done(((f32[576,2304]{1,0:T(8,128)}), f32[72,2304]{1,0:T(8,128)}) %reduce-scatter.2.cloned.1.call-update) | async-done | bytes 663568 | tf_op jit(solution)/shard_map/reduce_scatter | solution.py:44
  179.8 2.3 reshape.76
  182.2 0.9 copy.22
  183.1 18.4 %all_to_all.15 = f32[72,4,8,72]{0,2,3,1:T(8,128)S(1)} all-to-all(f32[72,4,8,72]{0,2,3,1:T(8,128)S(1)} %copy.22), channel_id=1, replica_groups=mesh['amp'=4,'own'=8] {'amp'}, dimensions={1} | all-to-all | bytes 1327104 | tf_op jit(solution)/shard_map/all_to_all | solution.py:53
  201.5 0.8 copy.23
  202.3 32.7 %all_to_all.16 = f32[72,4,8,72]{0,1,3,2:T(4,128)S(1)} all-to-all(f32[72,4,8,72]{0,1,3,2:T(4,128)S(1)} %copy.23), channel_id=1, replica_groups=mesh['amp'=4,'own'=8] {'own'}, dimensions={2} | all-to-all | bytes 1327104 | tf_op jit(solution)/shard_map/all_to_all | solution.py:52
  235.0 0.7 copy.24
  235.7 0.6 reshape.77
  236.3 0.8 add_convert_fusion
  (12 shorter events, 0.2 us)
Async XLA Ops:
  8.0 5.4 %copy-start.1 = (s32[18]{0:T(128)S(1)}, s32[18]{0:T(128)}, u32[]{:S(2)}) copy-start(s32[18]{0:T(128)} %param.7) | copy-start | bytes 220
  8.0 5.7 %copy-start.2 = (s32[34]{0:T(128)S(1)}, s32[34]{0:T(128)}, u32[]{:S(2)}) copy-start(s32[34]{0:T(128)} %param.6) | copy-start | bytes 412
  9.2 18.0 %all-to-all-start = ((bf16[4,4,576,48]{2,3,1,0:T(8,128)(2,1)}), bf16[4,4,576,48]{2,3,1,0:T(8,128)(2,1)S(1)}, u32[]{:S(2)}, u32[]{:S(2)}) async-start(bf16[4,4,576,48]{2,3,1,0:T(8,128)(2,1)} %pad_maximum_fusion), calls=%async_computation | async-start | bytes 1966080 | tf_op jit(solution)/shard_map/all_to_all | solution.py:24
  13.4 166.4 %reduce-scatter.2.cloned.1.call-start = ((), (), s32[]{:S(2)}) async-start(), calls=%async_computation.4 | async-start | bytes 5971968 | tf_op jit(solution)/shard_map/reduce_scatter | solution.py:44
  235.0 1.3 copy-start
Sparse Core Ops, SparseCore 0:
  74.6 105.1 reduce-scatter.1
